TPU v7x, 32 devices: a whole 2x2x4 slice. The times are simulated.
32 devices in a mesh: dp: 4 (over y, x), segment: 4 (over z), mp: 2 (over core).
Axes of the slice: x: 2, y: 2, z: 4, core: 2. Of those that a mesh axis runs over, the one named last changes fastest.
Arguments:
- trunk_in: bfloat16 [1024, 2560], P('dp', 'mp'), may hold values from -6 to 6
- norm_gain: bfloat16 [4, 2560], P('segment'), may hold values from 0.5 to 1.5
- w_gate: bfloat16 [4, 2560, 3584], P('segment', 'dp', 'mp'), may hold values from -0.125 to 0.125
- w_up: bfloat16 [4, 2560, 3584], P('segment', 'dp', 'mp'), may hold values from -0.125 to 0.125
- w_down: bfloat16 [4, 3584, 2560], P('segment', 'mp', 'dp'), may hold values from -0.09375 to 0.09375
- w_cond: bfloat16 [2560, 512], P('mp'), may hold values from -0.125 to 0.125
- w_time: bfloat16 [256, 512], replicated, may hold values from -0.375 to 0.375
- w_in: bfloat16 [70, 256], replicated, may hold values from -0.75 to 0.75
- w_mid: bfloat16 [1280, 256], replicated, may hold values from -0.15625 to 0.15625
- w_res: bfloat16 [14, 256], replicated, may hold values from -1.5 to 1.5
- w_out: bfloat16 [256, 14], replicated, may hold values from -0.375 to 0.375
- tsteps: int32 [64, 8], P('dp'), may hold values from 0 to 99
- advantage: float32 [64, 8], P('dp'), may hold values from -4 to 4
- actions: bfloat16 [64, 64, 14], P('dp'), may hold values from -6 to 6
- noise: bfloat16 [64, 8, 64, 14], P('dp'), may hold values from -6 to 6
Outputs:
- grad_w_in: float32 [70, 256], P(None, 'segment')
- grad_w_mid: float32 [1280, 256], P(None, 'segment')
- grad_w_res: float32 [14, 256], P(None, 'segment')
- grad_w_out: float32 [256, 14], P('segment')
- grad_w_time: float32 [256, 512], P(None, 'segment')
- grad_w_cond: float32 [2560, 512], P('mp', 'segment')
- grad_cond: float32 [64, 2560], P(('dp', 'segment'), 'mp')
- loss: float32 [1], replicated
All inputs are finite; a program needn't handle non-finite values.
Results may differ from a plain program's by a relative error of at most 0.035.
Values may be sent and summed in bfloat16 or wider, within the bound.
No kernel may reach another device: no remote copies, remote signals or barrier semaphores. Data moves between devices by JAX's collectives and lax.ppermute only.
A program may use at most 128 MiB of HBM per device.

v0:
```python
import math
import jax
import jax.numpy as jnp
from jax import lax
from jax.sharding import PartitionSpec as P

GROUPS = 8
TSTEPS = 100
TPS = 16
SPM = 4
SPD = 16
LEV = 8


def passed_along(block, axis, distance):
    devices = range(lax.axis_size(axis))
    route = [(i - distance, i) for i in devices if i - distance in devices]
    return lax.ppermute(block, axis, route)


def spread_2(value, axis, source):
    kept = jnp.where(lax.axis_index(axis) == source, value, 0).astype(value.dtype)
    return lax.psum(kept, axis)


def mish_value(values):
    return values * jnp.tanh(jax.nn.softplus(values))


def mish_slope(values):
    soft = jnp.tanh(jax.nn.softplus(values))
    return soft + values * jax.nn.sigmoid(values) * (1.0 - soft * soft)


def contract(form, left, right):
    return jnp.einsum(form, left, right, preferred_element_type=jnp.float32)


def alpha_table():
    grid = jnp.arange(TSTEPS + 1, dtype=jnp.float32) / TSTEPS
    curve = jnp.cos((grid + 0.008) / 1.008 * math.pi / 2.0) ** 2
    betas = jnp.minimum(1.0 - curve[1:] / curve[:-1], 0.999)
    return jnp.cumprod(1.0 - betas)


def norm_act(values):
    rows, steps, channels = values.shape
    grouped = values.reshape(rows, steps, GROUPS, channels // GROUPS)
    center = jnp.mean(grouped, axis=(1, 3), keepdims=True)
    spread = jnp.mean((grouped - center) ** 2, axis=(1, 3), keepdims=True)
    normed = (grouped - center) * lax.rsqrt(spread + 1e-05)
    return mish_value(normed.reshape(rows, steps, channels))


def columns(values):
    steps = values.shape[1]
    padded = jnp.pad(values, ((0, 0), (2, 2), (0, 0)))
    return jnp.concatenate([padded[:, tap : tap + steps] for tap in range(5)], axis=2)


def columns_adjoint(grads, width):
    total = 0.0
    for tap in range(5):
        piece = grads[:, :, tap * width : (tap + 1) * width]
        total = total + jnp.pad(piece, ((0, 0), (tap, 4 - tap), (0, 0)))
    return total[:, 2:-2]


def own_block(values, which, count, axis_number):
    width = values.shape[axis_number] // count
    return lax.dynamic_slice_in_dim(values, which * width, width, axis_number)


def denoise(
    film_cond, tsteps, advantage, actions, noise, w_in, w_mid, w_res, w_out, w_time, product
):
    row_count, levels = tsteps.shape
    horizon, action_dims = (actions.shape[1], actions.shape[2])
    channels = w_mid.shape[1]
    flat = row_count * levels
    matches = (tsteps[:, :, None] == jnp.arange(TSTEPS, dtype=jnp.int32)[None, None, :]).astype(
        jnp.float32
    )
    alpha = jnp.sum(matches * alpha_table()[None, None, :], axis=2)
    keep_root = jnp.sqrt(alpha)[:, :, None, None]
    noise_root = jnp.sqrt(1.0 - alpha)[:, :, None, None]
    noisy_act = (
        keep_root * actions.astype(jnp.float32)[:, None] + noise_root * noise.astype(jnp.float32)
    ).astype(jnp.bfloat16)
    noisy_act = noisy_act.reshape(flat, horizon, action_dims)
    half_dim = w_time.shape[0] // 2
    frequencies = jnp.exp(
        -math.log(10000.0) * jnp.arange(half_dim, dtype=jnp.float32) / (half_dim - 1)
    )
    angles = tsteps.astype(jnp.float32)[:, :, None] * frequencies[None, None, :]
    embedded = jnp.concatenate([jnp.sin(angles), jnp.cos(angles)], axis=2)
    time_act = mish_value(embedded).astype(jnp.bfloat16).reshape(flat, 2 * half_dim)
    film = film_cond[:, None, :] + product(
        "rld,dc->rlc", time_act.reshape(row_count, levels, -1), w_time
    )
    film = film.reshape(flat, 2 * channels)
    film_scale = film[:, None, :channels]
    film_shift = film[:, None, channels:]
    columns_in = columns(noisy_act)
    pre_first = product("mhk,kc->mhc", columns_in, w_in)
    act_first, first_back = jax.vjp(norm_act, pre_first)
    modulated = (film_scale * act_first + film_shift).astype(jnp.bfloat16)
    columns_mid = columns(modulated)
    pre_second = product("mhk,kc->mhc", columns_mid, w_mid)
    act_second, second_back = jax.vjp(norm_act, pre_second)
    block_out = (act_second + product("mha,ac->mhc", noisy_act, w_res)).astype(jnp.bfloat16)
    predicted = product("mhc,ca->mha", block_out, w_out)
    errors = predicted - noise.reshape(flat, horizon, action_dims).astype(jnp.float32)
    err_sum = jnp.sum(errors * errors) / (horizon * action_dims)
    weights = advantage.reshape(flat, 1, 1)
    d_pred = (2.0 * weights * errors / (horizon * action_dims)).astype(jnp.bfloat16)
    grad_out = product("mhc,mha->ca", block_out, d_pred)
    d_block = product("mha,ca->mhc", d_pred, w_out)
    grad_res = product("mha,mhc->ac", noisy_act, d_block.astype(jnp.bfloat16))
    d_second = second_back(d_block)[0].astype(jnp.bfloat16)
    grad_mid = product("mhk,mhc->kc", columns_mid, d_second)
    d_columns = product("mhc,kc->mhk", d_second, w_mid)
    d_modulated = columns_adjoint(d_columns, channels)
    d_film = jnp.concatenate(
        [jnp.sum(d_modulated * act_first, axis=1), jnp.sum(d_modulated, axis=1)], axis=1
    )
    d_first = first_back(film_scale * d_modulated)[0].astype(jnp.bfloat16)
    grad_in = product("mhk,mhc->kc", columns_in, d_first)
    grad_time = product("md,mc->dc", time_act, d_film.astype(jnp.bfloat16))
    d_film_cond = jnp.sum(d_film.reshape(row_count, levels, -1), axis=1)
    return (err_sum, grad_in, grad_mid, grad_res, grad_out, grad_time, d_film_cond)


def body(
    trunk_in,
    norm_gain,
    w_gate,
    w_up,
    w_down,
    w_cond,
    w_time,
    w_in,
    w_mid,
    w_res,
    w_out,
    tsteps,
    advantage,
    actions,
    noise,
):
    segments = lax.axis_size("segment")
    segment_index = lax.axis_index("segment")
    cores = lax.axis_size("mp")
    core_index = lax.axis_index("mp")
    gate_full, up_full, down_full = (
        lax.all_gather(w_gate, "dp", axis=1, tiled=True),
        lax.all_gather(w_up, "dp", axis=1, tiled=True),
        lax.all_gather(w_down, "dp", axis=2, tiled=True),
    )
    gate_weight = gate_full[0]
    up_weight = up_full[0]
    down_weight = down_full[0]
    norm_scale = norm_gain[0].astype(jnp.float32)
    micro_count = SPD // SPM
    batch_rows = SPM * TPS
    half_width = trunk_in.shape[1]
    inputs = trunk_in.reshape(micro_count, batch_rows, half_width)

    def trunk_layer(current):
        whole_rows = lax.all_gather(current, "mp", axis=1, tiled=True)
        widened = whole_rows.astype(jnp.float32)
        factor = lax.rsqrt(jnp.mean(widened * widened, axis=1, keepdims=True) + 1e-05)
        normed = (widened * factor * norm_scale).astype(jnp.bfloat16)
        gate_out = jnp.dot(normed, gate_weight, preferred_element_type=jnp.float32)
        up_out = jnp.dot(normed, up_weight, preferred_element_type=jnp.float32)
        hidden = (jax.nn.silu(gate_out) * up_out).astype(jnp.bfloat16)
        partial_out = jnp.dot(hidden, down_weight, preferred_element_type=jnp.float32)
        summed = lax.psum_scatter(
            partial_out.astype(jnp.bfloat16), "mp", scatter_dimension=1, tiled=True
        ).astype(jnp.float32)
        return (current.astype(jnp.float32) + summed).astype(jnp.bfloat16)

    def advance(step_index, loop_state):
        received, stored = loop_state
        fresh_rows = lax.dynamic_index_in_dim(
            inputs, jnp.minimum(step_index, micro_count - 1), 0, keepdims=False
        )
        fresh_rows = jnp.where(step_index < micro_count, fresh_rows, jnp.zeros_like(fresh_rows))
        current = jnp.where(segment_index == 0, fresh_rows, received)
        result = trunk_layer(current)
        slot_index = jnp.clip(step_index - (segments - 1), 0, micro_count - 1)
        previous = lax.dynamic_index_in_dim(stored, slot_index, 0, keepdims=False)
        kept_rows = jnp.where(step_index >= segments - 1, result, previous)
        stored = lax.dynamic_update_index_in_dim(stored, kept_rows, slot_index, 0)
        received = passed_along(result, "segment", 1)
        return (received, stored)

    start_state = (
        jnp.zeros((batch_rows, half_width), jnp.bfloat16),
        jnp.zeros((micro_count, batch_rows, half_width), jnp.bfloat16),
    )
    final_state = lax.fori_loop(0, micro_count + segments - 1, advance, start_state)
    trunk_out = final_state[1].reshape(SPD, TPS, half_width)
    cond = jnp.mean(trunk_out.astype(jnp.float32), axis=1).astype(jnp.bfloat16)
    is_last = (segment_index == segments - 1).astype(jnp.float32)
    row_total = cond.shape[0]
    own_rows = row_total // cores
    cond_act = mish_value(cond.astype(jnp.float32)).astype(jnp.bfloat16)
    film_cond = lax.psum_scatter(
        jnp.dot(cond_act, w_cond, preferred_element_type=jnp.float32).astype(jnp.bfloat16),
        "mp",
        scatter_dimension=0,
        tiled=True,
    ).astype(jnp.float32)
    begin_row = core_index * own_rows
    steps_own = lax.dynamic_slice_in_dim(tsteps, begin_row, own_rows, 0)
    advantage_own = lax.dynamic_slice_in_dim(advantage, begin_row, own_rows, 0)
    actions_own = lax.dynamic_slice_in_dim(actions, begin_row, own_rows, 0)
    noise_own = lax.dynamic_slice_in_dim(noise, begin_row, own_rows, 0)
    outcome = denoise(
        film_cond,
        steps_own,
        advantage_own,
        actions_own,
        noise_own,
        w_in,
        w_mid,
        w_res,
        w_out,
        w_time,
        contract,
    )
    err_sum, grad_in, grad_mid, grad_res, grad_out, grad_time, d_film_cond = outcome
    film_share = (d_film_cond * is_last).astype(jnp.bfloat16)
    film_all = lax.all_gather(film_share, "mp", axis=0, tiled=True)
    cond_grad_part = contract("sc,dc->sd", film_all, w_cond) * mish_slope(cond.astype(jnp.float32))
    grad_cond = lax.psum_scatter(
        cond_grad_part.astype(jnp.bfloat16), "segment", scatter_dimension=0, tiled=True
    ).astype(jnp.float32)
    local_sums = (
        lax.psum(grad_in.astype(jnp.bfloat16), ("dp", "mp")).astype(jnp.float32),
        lax.psum(grad_mid.astype(jnp.bfloat16), ("dp", "mp")).astype(jnp.float32),
        lax.psum(grad_res.astype(jnp.bfloat16), ("dp", "mp")).astype(jnp.float32),
        lax.psum(grad_out.astype(jnp.bfloat16), ("dp", "mp")).astype(jnp.float32),
        lax.psum(grad_time.astype(jnp.bfloat16), ("dp", "mp")).astype(jnp.float32),
        lax.psum(err_sum.astype(jnp.bfloat16), ("dp", "mp")).astype(jnp.float32),
    )
    act_rows, grad_rows = (
        lax.all_gather(cond_act, "dp", axis=0, tiled=True),
        lax.all_gather(film_all, "dp", axis=0, tiled=True),
    )
    local_cond = contract("sd,sc->dc", act_rows, grad_rows)
    fanned = (
        spread_2(local_sums[0].astype(jnp.bfloat16), "segment", segments - 1).astype(jnp.float32),
        spread_2(local_sums[1].astype(jnp.bfloat16), "segment", segments - 1).astype(jnp.float32),
        spread_2(local_sums[2].astype(jnp.bfloat16), "segment", segments - 1).astype(jnp.float32),
        spread_2(local_sums[3].astype(jnp.bfloat16), "segment", segments - 1).astype(jnp.float32),
        spread_2(local_sums[4].astype(jnp.bfloat16), "segment", segments - 1).astype(jnp.float32),
        spread_2(local_sums[5].astype(jnp.bfloat16), "segment", segments - 1).astype(jnp.float32),
        spread_2(local_cond.astype(jnp.bfloat16), "segment", segments - 1).astype(local_cond.dtype),
    )
    summed_grads = fanned[:6]
    grad_w_cond = own_block(fanned[6], segment_index, segments, 1)
    replicas = lax.axis_size("dp")
    loss = (summed_grads[5] / (replicas * SPD * LEV)).reshape(1)
    return (
        own_block(summed_grads[0], segment_index, segments, 1),
        own_block(summed_grads[1], segment_index, segments, 1),
        own_block(summed_grads[2], segment_index, segments, 1),
        own_block(summed_grads[3], segment_index, segments, 0),
        own_block(summed_grads[4], segment_index, segments, 1),
        grad_w_cond,
        grad_cond,
        loss,
    )


def solution(mesh):
    in_specs = (
        P("dp", "mp"),
        P("segment", None),
        P("segment", "dp", "mp"),
        P("segment", "dp", "mp"),
        P("segment", "mp", "dp"),
        P("mp", None),
        P(),
        P(),
        P(),
        P(),
        P(),
        P("dp", None),
        P("dp", None),
        P("dp", None, None),
        P("dp", None, None, None),
    )
    out_specs = (
        P(None, "segment"),
        P(None, "segment"),
        P(None, "segment"),
        P("segment", None),
        P(None, "segment"),
        P("mp", "segment"),
        P(("dp", "segment"), "mp"),
        P(),
    )
    return jax.shard_map(body, mesh=mesh, in_specs=in_specs, out_specs=out_specs, check_vma=False)
```

profile of v0, /device:TPU:0, one launch (start us, length us, event | category | flops | bytes accessed | tf_op | source)
XLA Modules:
  0.0 852.6 jit_solution(11993340985135364638)
XLA Ops:
  14.4 6.5 concatenate.15
  20.9 4.2 fusion.91
  31.5 75.1 %all-gather.4.cloned.1.call-done = bf16[1,2560,1792]{2,1,0:T(8,128)(2,1)} async-done(((bf16[1,640,1792]{2,1,0:T(8,128)(2,1)}), bf16[1,2560,1792]{2,1,0:T(8,128)(2,1)}) %all-gather.4.cloned.1.call-update) | async-done | bytes 9175056 | tf_op jit(solution)/shard_map/all_gather | solution.py:156
  106.6 95.9 %all-gather.6.cloned.1.call-done = bf16[1,2560,1792]{2,1,0:T(8,128)(2,1)} async-done(((bf16[1,640,1792]{2,1,0:T(8,128)(2,1)}), bf16[1,2560,1792]{2,1,0:T(8,128)(2,1)}) %all-gather.6.cloned.1.call-update) | async-done | bytes 9175056 | tf_op jit(solution)/shard_map/all_gather | solution.py:157
  202.5 95.9 %all-gather.8.cloned.1.call-done = bf16[1,1792,2560]{2,1,0:T(8,128)(2,1)} async-done(((bf16[1,1792,640]{2,1,0:T(8,128)(2,1)}), bf16[1,1792,2560]{2,1,0:T(8,128)(2,1)}) %all-gather.8.cloned.1.call-update) | async-done | bytes 9175056 | tf_op jit(solution)/shard_map/all_gather | solution.py:158
  299.3 263.3 %while.17 = (s32[]{:T(128)}, bf16[64,1280]{1,0:T(8,128)(2,1)S(1)}, bf16[4,64,1280]{2,1,0:T(8,128)(2,1)}, pred[]{:T(512)}, bf16[4,64,1280]{2,1,0:T(8,128)(2,1)}, ...) while((s32[]{:T(128)}, bf16[64,1280]{1,0:T(8,128)(2,1)S(1)}, ...), condition=%wide.region_5.6_spmd, body=%wide.region_2.5_spmd.sunk | while | flops 1764835328 | bytes 34035272 | solution.py:202
  302.5 5.4 fusion.126
  307.9 10.3 %convolution_convert_fusion.5 = bf16[64,2560]{1,0:T(8,128)(2,1)} fusion(bf16[1792,2560]{1,0:T(8,128)(2,1)} %get-tuple-element.408, bf16[2560,1792]{1,0:T(8,128)(2,1)} %get-tuple-element.407, f32[64,1792]{1,0:T(8,128)S(1)} %fusion.126, bf16[64,2560]{1,0:T(8,128)(2,1)S(1)} %all_gather.35, f32[2560]{0:T(1024)S(1)} %get-tuple-element.405, ...), kind=kOutput, calls=%fused_computation.clone.1 | convolution fusion | flops 1175912448 | bytes 19474688 | tf_op jit(solution)/shard_map/while/body/eval_jaxpr/dot_general | solution.py:177
  319.2 7.0 reduce-scatter.5.cloned.1.call-done
  331.4 4.0 collective-permute-done
  338.5 5.4 fusion.126
  343.9 10.3 %convolution_convert_fusion.5 = bf16[64,2560]{1,0:T(8,128)(2,1)} fusion(bf16[1792,2560]{1,0:T(8,128)(2,1)} %get-tuple-element.408, bf16[2560,1792]{1,0:T(8,128)(2,1)} %get-tuple-element.407, f32[64,1792]{1,0:T(8,128)S(1)} %fusion.126, bf16[64,2560]{1,0:T(8,128)(2,1)S(1)} %all_gather.35, f32[2560]{0:T(1024)S(1)} %get-tuple-element.405, ...), kind=kOutput, calls=%fused_computation.clone.1 | convolution fusion | flops 1175912448 | bytes 19474688 | tf_op jit(solution)/shard_map/while/body/eval_jaxpr/dot_general | solution.py:177
  355.1 8.9 %reduce-scatter.5.cloned.1.call-done = bf16[64,1280]{1,0:T(8,128)(2,1)} async-done(((bf16[64,2560]{1,0:T(8,128)(2,1)}), bf16[64,1280]{1,0:T(8,128)(2,1)}) %reduce-scatter.5.cloned.1.call-update) | async-done | bytes 163856 | tf_op jit(solution)/shard_map/while/body/eval_jaxpr/reduce_scatter | solution.py:178
  369.3 3.9 collective-permute-done
  376.4 5.4 fusion.126
  381.8 10.3 %convolution_convert_fusion.5 = bf16[64,2560]{1,0:T(8,128)(2,1)} fusion(bf16[1792,2560]{1,0:T(8,128)(2,1)} %get-tuple-element.408, bf16[2560,1792]{1,0:T(8,128)(2,1)} %get-tuple-element.407, f32[64,1792]{1,0:T(8,128)S(1)} %fusion.126, bf16[64,2560]{1,0:T(8,128)(2,1)S(1)} %all_gather.35, f32[2560]{0:T(1024)S(1)} %get-tuple-element.405, ...), kind=kOutput, calls=%fused_computation.clone.1 | convolution fusion | flops 1175912448 | bytes 19474688 | tf_op jit(solution)/shard_map/while/body/eval_jaxpr/dot_general | solution.py:177
  393.0 8.9 %reduce-scatter.5.cloned.1.call-done = bf16[64,1280]{1,0:T(8,128)(2,1)} async-done(((bf16[64,2560]{1,0:T(8,128)(2,1)}), bf16[64,1280]{1,0:T(8,128)(2,1)}) %reduce-scatter.5.cloned.1.call-update) | async-done | bytes 163856 | tf_op jit(solution)/shard_map/while/body/eval_jaxpr/reduce_scatter | solution.py:178
  407.2 3.9 collective-permute-done
  414.3 5.4 fusion.126
  419.7 10.3 %convolution_convert_fusion.5 = bf16[64,2560]{1,0:T(8,128)(2,1)} fusion(bf16[1792,2560]{1,0:T(8,128)(2,1)} %get-tuple-element.408, bf16[2560,1792]{1,0:T(8,128)(2,1)} %get-tuple-element.407, f32[64,1792]{1,0:T(8,128)S(1)} %fusion.126, bf16[64,2560]{1,0:T(8,128)(2,1)S(1)} %all_gather.35, f32[2560]{0:T(1024)S(1)} %get-tuple-element.405, ...), kind=kOutput, calls=%fused_computation.clone.1 | convolution fusion | flops 1175912448 | bytes 19474688 | tf_op jit(solution)/shard_map/while/body/eval_jaxpr/dot_general | solution.py:177
  430.9 8.9 %reduce-scatter.5.cloned.1.call-done = bf16[64,1280]{1,0:T(8,128)(2,1)} async-done(((bf16[64,2560]{1,0:T(8,128)(2,1)}), bf16[64,1280]{1,0:T(8,128)(2,1)}) %reduce-scatter.5.cloned.1.call-update) | async-done | bytes 163856 | tf_op jit(solution)/shard_map/while/body/eval_jaxpr/reduce_scatter | solution.py:178
  445.1 3.9 collective-permute-done
  452.2 5.4 fusion.126
  457.5 10.3 %convolution_convert_fusion.5 = bf16[64,2560]{1,0:T(8,128)(2,1)} fusion(bf16[1792,2560]{1,0:T(8,128)(2,1)} %get-tuple-element.408, bf16[2560,1792]{1,0:T(8,128)(2,1)} %get-tuple-element.407, f32[64,1792]{1,0:T(8,128)S(1)} %fusion.126, bf16[64,2560]{1,0:T(8,128)(2,1)S(1)} %all_gather.35, f32[2560]{0:T(1024)S(1)} %get-tuple-element.405, ...), kind=kOutput, calls=%fused_computation.clone.1 | convolution fusion | flops 1175912448 | bytes 19474688 | tf_op jit(solution)/shard_map/while/body/eval_jaxpr/dot_general | solution.py:177
  468.8 8.9 %reduce-scatter.5.cloned.1.call-done = bf16[64,1280]{1,0:T(8,128)(2,1)} async-done(((bf16[64,2560]{1,0:T(8,128)(2,1)}), bf16[64,1280]{1,0:T(8,128)(2,1)}) %reduce-scatter.5.cloned.1.call-update) | async-done | bytes 163856 | tf_op jit(solution)/shard_map/while/body/eval_jaxpr/reduce_scatter | solution.py:178
  483.0 3.9 collective-permute-done
  490.0 5.4 fusion.126
  495.4 10.3 %convolution_convert_fusion.5 = bf16[64,2560]{1,0:T(8,128)(2,1)} fusion(bf16[1792,2560]{1,0:T(8,128)(2,1)} %get-tuple-element.408, bf16[2560,1792]{1,0:T(8,128)(2,1)} %get-tuple-element.407, f32[64,1792]{1,0:T(8,128)S(1)} %fusion.126, bf16[64,2560]{1,0:T(8,128)(2,1)S(1)} %all_gather.35, f32[2560]{0:T(1024)S(1)} %get-tuple-element.405, ...), kind=kOutput, calls=%fused_computation.clone.1 | convolution fusion | flops 1175912448 | bytes 19474688 | tf_op jit(solution)/shard_map/while/body/eval_jaxpr/dot_general | solution.py:177
  506.7 8.9 %reduce-scatter.5.cloned.1.call-done = bf16[64,1280]{1,0:T(8,128)(2,1)} async-done(((bf16[64,2560]{1,0:T(8,128)(2,1)}), bf16[64,1280]{1,0:T(8,128)(2,1)}) %reduce-scatter.5.cloned.1.call-update) | async-done | bytes 163856 | tf_op jit(solution)/shard_map/while/body/eval_jaxpr/reduce_scatter | solution.py:178
  527.9 5.4 fusion.126
  533.3 10.3 %convolution_convert_fusion.5 = bf16[64,2560]{1,0:T(8,128)(2,1)} fusion(bf16[1792,2560]{1,0:T(8,128)(2,1)} %get-tuple-element.408, bf16[2560,1792]{1,0:T(8,128)(2,1)} %get-tuple-element.407, f32[64,1792]{1,0:T(8,128)S(1)} %fusion.126, bf16[64,2560]{1,0:T(8,128)(2,1)S(1)} %all_gather.35, f32[2560]{0:T(1024)S(1)} %get-tuple-element.405, ...), kind=kOutput, calls=%fused_computation.clone.1 | convolution fusion | flops 1175912448 | bytes 19474688 | tf_op jit(solution)/shard_map/while/body/eval_jaxpr/dot_general | solution.py:177
  544.6 8.9 %reduce-scatter.5.cloned.1.call-done = bf16[64,1280]{1,0:T(8,128)(2,1)} async-done(((bf16[64,2560]{1,0:T(8,128)(2,1)}), bf16[64,1280]{1,0:T(8,128)(2,1)}) %reduce-scatter.5.cloned.1.call-update) | async-done | bytes 163856 | tf_op jit(solution)/shard_map/while/body/eval_jaxpr/reduce_scatter | solution.py:178
  570.3 9.4 %all_gather.31 = bf16[64,1280]{1,0:T(8,128)(2,1)} all-gather(bf16[16,1280]{1,0:T(8,128)(2,1)S(1)} %fusion.57), channel_id=1, replica_groups=mesh['dp'=4,'segment'=4,'mp'=2] {'dp'}, dimensions={0}, use_global_device_ids=true | all-gather | bytes 204800 | tf_op jit(solution)/shard_map/all_gather | solution.py:249
  581.6 4.7 add_convert_fusion.3
  594.1 5.3 fusion.92
  603.0 5.2 fusion.28
  610.4 7.9 multiply_reduce_fusion.8
  622.2 5.0 add_convert_fusion.2
  627.3 7.8 fusion.30
  635.1 8.6 %fusion.45 = f32[64,64,1280]{2,1,0:T(8,128)} fusion(bf16[64,64,256]{2,1,0:T(8,128)(2,1)S(1)} %add_convert_fusion.2, bf16[1280,256]{1,0:T(8,128)(2,1)S(1)} %copy-done.12), kind=kOutput, calls=%fused_computation.87 | convolution fusion | flops 2684354560 | bytes 23724032 | tf_op jit(solution)/shard_map/mhc,kc->mhk/dot_general | solution.py:36
  643.7 12.7 %fusion.88 = (f32[64,64,256]{2,1,0:T(8,128)S(1)}, f32[64,64,256]{2,1,0:T(8,128)S(1)}, f32[64,64,256]{2,1,0:T(8,128)}, f32[64,64,256]{2,1,0:T(8,128)}, f32[64,64,256]{2,1,0:T(8,128)}) fusion(f32[64,64,1280]{2,1,0:T(8,128)} %fusion.45), kind=kLoop, calls=%fused_computation.189 | loop fusion | bytes 41943040 | tf_op jit(solution)/shard_map/slice | solution.py:64
  656.4 13.4 %multiply_reduce_fusion = (f32[64,256]{1,0:T(8,128)S(1)}, f32[64,256]{1,0:T(8,128)S(1)}, f32[64,256]{1,0:T(8,128)}, f32[64,256]{1,0:T(8,128)S(1)}, f32[64,64,256]{2,1,0:T(8,128)}) fusion(f32[64,256]{1,0:T(8,128)S(1)} %copy.102, f32[64,64,256]{2,1,0:T(8,128)S(1)} %copy-done.2, f32[64,256]{1,0:T(8,128)S(1)} %copy.100, f32[64,256]{1,0:T(8,128)S(1)} %copy-done.8, ...), kind=kLoop, calls=%fused_computation.42 | loop fusion | flops 35586048 | bytes 29818880 | tf_op jit(solution)/shard_map/reduce_sum | solution.py:125
  671.8 8.4 all_gather.33
  693.8 49.4 %all-reduce.16.cloned.1.call-done = (bf16[1280,256]{0,1:T(8,128)(2,1)}, bf16[256,512]{1,0:T(8,128)(2,1)}) async-done(((bf16[1280,256]{0,1:T(8,128)(2,1)}, bf16[256,512]{1,0:T(8,128)(2,1)}), (bf16[1280,256]{0,1:T(8,128)(2,1)}, bf16[256,512]{1,0:T(8,128)(2,1)})) %all-reduce.16.cloned.1.call-update) | async-done | bytes 917520 | tf_op jit(solution)/shard_map/psum | solution.py:242
  745.6 4.8 fusion.37
  750.4 24.5 %all-reduce.8 = (bf16[70,256]{0,1:T(8,128)(2,1)S(1)}, bf16[14,256]{1,0:T(8,128)(2,1)S(1)}, bf16[256,14]{0,1:T(8,128)(2,1)S(1)}, bf16[]{:T(256)}) all-reduce(bf16[70,256]{0,1:T(8,128)(2,1)S(1)} %fusion.37, bf16[14,256]{1,0:T(8,128)(2,1)S(1)} %copy-done.25, ...), channel_id=1, replica_groups=mesh['dp'=4,'segment'=4,'mp'=2] {'dp','mp'}, use_global_device_ids=true, to_apply=%region_28.30 | all-reduce | flops 25089 | bytes 100356 | tf_op jit(solution)/shard_map/psum | solution.py:241
  776.1 26.0 %all-reduce.19 = (bf16[70,256]{0,1:T(8,128)(2,1)S(1)}, bf16[14,256]{1,0:T(8,128)(2,1)S(1)}, bf16[256,14]{0,1:T(8,128)(2,1)S(1)}, bf16[16,1280]{1,0:T(8,128)(2,1)S(1)}, bf16[]{:T(256)}) all-reduce(bf16[70,256]{0,1:T(8,128)(2,1)S(1)} %broadcast_select_fusion.2, ...), channel_id=1, replica_groups=mesh['dp'=4,'segment'=4,'mp'=2] {'segment'}, use_global_device_ids=true, to_apply=%region_29.31 | all-reduce | flops 45569 | bytes 182276 | tf_op jit(solution)/shard_map/psum | solution.py:23
  805.3 34.1 %all-reduce.18.cloned.1.call-done = (bf16[1280,256]{0,1:T(8,128)(2,1)}, bf16[256,512]{1,0:T(8,128)(2,1)}, bf16[1280,512]{1,0:T(8,128)(2,1)}) async-done(((bf16[1280,256]{0,1:T(8,128)(2,1)}, bf16[256,512]{1,0:T(8,128)(2,1)}, bf16[1280,512]{1,0:T(8,128)(2,1)}), (bf16[1280,256]{0,1:T(8,128)(2,1)}, bf16[256,512]{1,0:T(8,128)(2,1)}, bf16[1280,512]{1,0:T(8,128)(2,1)})) %all-reduce.18.cloned.1.call-update) | async-done | bytes 2228240 | tf_op jit(solution)/shard_map/psum | solution.py:23
  (249 shorter events, 138.9 us)
Async XLA Ops:
  7.2 556.9 %copy-start = (bf16[1280,512]{1,0:T(8,128)(2,1)S(1)}, bf16[1280,512]{1,0:T(8,128)(2,1)}, u32[]{:S(2)}) copy-start(bf16[1280,512]{1,0:T(8,128)(2,1)} %param.23) | copy-start | bytes 3932164
  7.2 2.8 copy-start.26
  7.2 3.3 copy-start.15
  7.2 99.4 %all-gather.4.cloned.1.call-start = ((), (), s32[]{:S(2)}) async-start(), calls=%async_computation.2 | async-start | bytes 11468800 | tf_op jit(solution)/shard_map/all_gather | solution.py:156
  7.9 194.6 %all-gather.6.cloned.1.call-start = ((), (), s32[]{:S(2)}) async-start(), calls=%async_computation.3 | async-start | bytes 11468800 | tf_op jit(solution)/shard_map/all_gather | solution.py:157
  8.7 289.7 %all-gather.8.cloned.1.call-start = ((), (), s32[]{:S(2)}) async-start(), calls=%async_computation.4 | async-start | bytes 11468800 | tf_op jit(solution)/shard_map/all_gather | solution.py:158
  11.2 591.8 %copy-start.4 = (bf16[8,8,64,14]{3,2,1,0:T(8,128)(2,1)}, bf16[8,8,64,14]{3,2,1,0:T(8,128)(2,1)S(1)}, u32[]{:S(2)}) copy-start(bf16[8,8,64,14]{3,2,1,0:T(8,128)(2,1)S(1)} %copy.96) | copy-start | bytes 344068
  14.4 6.5 copy-start.24
  20.8 7.6 copy-start.27
  299.3 26.8 %reduce-scatter.5.cloned.1.call-start = ((), (), s32[]{:S(2)}) async-start(), calls=%async_computation.8 | async-start | bytes 491520 | tf_op jit(solution)/shard_map/while/body/eval_jaxpr/reduce_scatter | solution.py:178
  327.8 7.6 collective-permute-start
  335.3 28.7 %reduce-scatter.5.cloned.1.call-start = ((), (), s32[]{:S(2)}) async-start(), calls=%async_computation.8 | async-start | bytes 491520 | tf_op jit(solution)/shard_map/while/body/eval_jaxpr/reduce_scatter | solution.py:178
  365.7 7.5 collective-permute-start
  373.2 28.7 %reduce-scatter.5.cloned.1.call-start = ((), (), s32[]{:S(2)}) async-start(), calls=%async_computation.8 | async-start | bytes 491520 | tf_op jit(solution)/shard_map/while/body/eval_jaxpr/reduce_scatter | solution.py:178
  403.6 7.5 collective-permute-start
  411.1 28.7 %reduce-scatter.5.cloned.1.call-start = ((), (), s32[]{:S(2)}) async-start(), calls=%async_computation.8 | async-start | bytes 491520 | tf_op jit(solution)/shard_map/while/body/eval_jaxpr/reduce_scatter | solution.py:178
  441.5 7.5 collective-permute-start
  449.0 28.7 %reduce-scatter.5.cloned.1.call-start = ((), (), s32[]{:S(2)}) async-start(), calls=%async_computation.8 | async-start | bytes 491520 | tf_op jit(solution)/shard_map/while/body/eval_jaxpr/reduce_scatter | solution.py:178
  479.4 7.5 collective-permute-start
  486.9 28.7 %reduce-scatter.5.cloned.1.call-start = ((), (), s32[]{:S(2)}) async-start(), calls=%async_computation.8 | async-start | bytes 491520 | tf_op jit(solution)/shard_map/while/body/eval_jaxpr/reduce_scatter | solution.py:178
  517.2 7.5 collective-permute-start
  524.8 28.7 %reduce-scatter.5.cloned.1.call-start = ((), (), s32[]{:S(2)}) async-start(), calls=%async_computation.8 | async-start | bytes 491520 | tf_op jit(solution)/shard_map/while/body/eval_jaxpr/reduce_scatter | solution.py:178
  555.1 7.5 collective-permute-start
  562.7 17.0 %reduce-scatter.3.cloned.1.call-start = ((), (), s32[]{:S(2)}) async-start(), calls=%async_computation.5 | async-start | bytes 24576 | tf_op jit(solution)/shard_map/reduce_scatter | solution.py:209
  564.0 16.4 %copy-start.9 = (f32[16,1280]{1,0:T(8,128)}, f32[16,1280]{1,0:T(8,128)S(1)}, u32[]{:S(2)}) copy-start(f32[16,1280]{1,0:T(8,128)S(1)} %convert_reduce_fusion) | copy-start | bytes 245764
  565.0 178.2 %all-reduce.16.cloned.1.call-start = ((), (), s32[]{:S(2)}) async-start(), calls=%async_computation.6 | async-start | bytes 1835008 | tf_op jit(solution)/shard_map/psum | solution.py:242
  581.6 6.7 copy-start.7
  591.7 2.3 copy-start.11
  594.1 5.3 copy-start.16
  599.4 3.5 copy-start.31
  602.9 5.2 copy-start.17
  603.0 5.2 copy-start.28
  603.0 6.8 copy-start.30
  627.3 7.8 copy-start.12
  643.7 12.7 %copy-start.2 = (f32[64,64,256]{2,1,0:T(8,128)S(1)}, f32[64,64,256]{2,1,0:T(8,128)}, u32[]{:S(2)}) copy-start(f32[64,64,256]{2,1,0:T(8,128)} %get-tuple-element.301) | copy-start | bytes 12582916
  643.7 12.7 %copy-start.8 = (f32[64,256]{1,0:T(8,128)S(1)}, f32[64,256]{1,0:T(8,128)}, u32[]{:S(2)}) copy-start(f32[64,256]{1,0:T(8,128)} %copy-done.7) | copy-start | bytes 196612
  669.8 15.0 %copy-start.22 = (f32[64,128]{1,0:T(8,128)S(1)}, f32[64,128]{1,0:T(8,128)}, u32[]{:S(2)}) copy-start(f32[64,128]{1,0:T(8,128)} %get-tuple-element.298) | copy-start | bytes 98308
  669.8 15.0 %copy-start.23 = (f32[64,128]{1,0:T(8,128)S(1)}, f32[64,128]{1,0:T(8,128)}, u32[]{:S(2)}) copy-start(f32[64,128]{1,0:T(8,128)} %get-tuple-element.299) | copy-start | bytes 98308
  669.8 16.0 %copy-start.19 = (bf16[64,1280]{1,0:T(8,128)(2,1)S(1)}, bf16[64,1280]{1,0:T(8,128)(2,1)}, u32[]{:S(2)}) copy-start(bf16[64,1280]{1,0:T(8,128)(2,1)} %all_gather.31) | copy-start | bytes 491524
  671.8 14.0 %copy-start.20 = (bf16[16,512]{1,0:T(8,128)(2,1)}, bf16[16,512]{1,0:T(8,128)(2,1)S(1)}, u32[]{:S(2)}) copy-start(bf16[16,512]{1,0:T(8,128)(2,1)S(1)} %all_gather.32) | copy-start | bytes 49156
  680.5 5.3 copy-start.13
  680.6 10.5 %copy-start.5 = (bf16[8,8,64,14]{3,2,1,0:T(8,128)(2,1)S(1)}, bf16[8,8,64,14]{3,2,1,0:T(8,128)(2,1)}, u32[]{:S(2)}) copy-start(bf16[8,8,64,14]{3,2,1,0:T(8,128)(2,1)} %copy-done.4) | copy-start | bytes 344068
  685.8 153.6 %all-reduce.18.cloned.1.call-start = ((), (), s32[]{:S(2)}) async-start(), calls=%async_computation.7 | async-start | bytes 4456448 | tf_op jit(solution)/shard_map/psum | solution.py:23
  687.5 58.1 %copy-start.6 = (bf16[64,64,70]{2,1,0:T(8,128)(2,1)S(1)}, bf16[64,64,70]{2,1,0:T(8,128)(2,1)}, u32[]{:S(2)}) copy-start(bf16[64,64,70]{2,1,0:T(8,128)(2,1)} %concatenate.15) | copy-start | bytes 1720324
  693.8 51.8 %copy-start.14 = (f32[64,256]{1,0:T(8,128)S(1)}, f32[64,256]{1,0:T(8,128)}, u32[]{:S(2)}) copy-start(f32[64,256]{1,0:T(8,128)} %copy-done.13) | copy-start | bytes 196612
  745.6 4.8 copy-start.25
  745.6 30.0 %copy-start.10 = (f32[16,1280]{1,0:T(8,128)S(1)}, f32[16,1280]{1,0:T(8,128)}, u32[]{:S(2)}) copy-start(f32[16,1280]{1,0:T(8,128)} %copy-done.9) | copy-start | bytes 245764
  745.6 30.0 %copy-start.21 = (bf16[16,512]{1,0:T(8,128)(2,1)S(1)}, bf16[16,512]{1,0:T(8,128)(2,1)}, u32[]{:S(2)}) copy-start(bf16[16,512]{1,0:T(8,128)(2,1)} %copy-done.20) | copy-start | bytes 49156
  (4 other events, 8.8 us)
Sparse Core Ops, SparseCore 0:
  9.9 96.7 all-gather.3
  108.5 94.0 all-gather.5
  204.4 94.0 all-gather.7
  318.3 7.7 reduce-scatter.4
  354.3 9.6 reduce-scatter.4
  392.2 9.6 reduce-scatter.4
  430.1 9.6 reduce-scatter.4
  468.0 9.6 reduce-scatter.4
  505.9 9.6 reduce-scatter.4
  543.8 9.6 reduce-scatter.4
  566.2 9.4 reduce-scatter.2
  685.9 57.1 all-reduce.15
  746.3 93.0 all-reduce.17
where the time goes:
time: 862 us; the launch traced here: 853 us
  waiting for transfers between devices  440 us (51%)
  matrix products  163 us (19%)
  blocking collectives  84.6 us (10%)
  other arithmetic  76.7 us (9%)
  local copies, waits for them, and re-layouts  42.8 us (5%)
  starting transfers between devices  25.4 us (3%)
  between operations  18.9 us (2%)
    all_gather x1, waiting for transfers between devices, body(): lax.all_gather(w_down, 'dp', axis=2, tiled=True)  95.9 us
    all_gather x1, waiting for transfers between devices, body(): lax.all_gather(w_up, 'dp', axis=1, tiled=True)  95.9 us
    all_gather x1, waiting for transfers between devices, body(): lax.all_gather(w_gate, 'dp', axis=1, tiled=True)  75.1 us
    dot_general x7, matrix products, trunk_layer(): jnp.dot(hidden, down_weight, preferred_element_type=jnp.float32)  72.1 us
    reduce_scatter x7, waiting for transfers between devices, trunk_layer(): lax.psum_scatter(partial_out.astype(jnp.bfloat16), 'mp', scatter_dimensio...  60.3 us
    dot_general x14, matrix products, contract(): return jnp.einsum(form, left, right, preferred_element_type=jnp.float32)  52.7 us
    psum x1, waiting for transfers between devices, body(): lax.psum(grad_mid.astype(jnp.bfloat16), ('dp', 'mp')).astype(jnp.float32)  49.4 us
    dot_general x7, matrix products, trunk_layer(): gate_out = jnp.dot(normed, gate_weight, preferred_element_type=jnp.float32)  37.6 us
  transfers between devices with their start and end apart: 20, of which 19 were waited for; matrix products, arithmetic and copies ran while one was open for 6% of the time, Pallas kernels for 0%

commit v1 on v0

--- a/solution.py
+++ b/solution.py
@@ -239,7 +239,7 @@
     ).astype(jnp.float32)
     local_sums = (
         lax.psum(grad_in.astype(jnp.bfloat16), ("dp", "mp")).astype(jnp.float32),
-        lax.psum(grad_mid.astype(jnp.bfloat16), ("dp", "mp")).astype(jnp.float32),
+        lax.psum(lax.psum(grad_mid.astype(jnp.bfloat16), "mp"), "dp").astype(jnp.float32),
         lax.psum(grad_res.astype(jnp.bfloat16), ("dp", "mp")).astype(jnp.float32),
         lax.psum(grad_out.astype(jnp.bfloat16), ("dp", "mp")).astype(jnp.float32),
         lax.psum(grad_time.astype(jnp.bfloat16), ("dp", "mp")).astype(jnp.float32),

time: 862 us -> 914 us (1.060)
  waiting for transfers between devices: 440 us -> 490 us
    psum x1 -> x3, waiting for transfers between devices: 49.4 us -> 97.1 us  [the longest x1 48.8 us: body(): lax.psum(grad_time.astype(jnp.bfloat16), ('dp', 'mp')).astype(jnp.float32)]
  transfers between devices with their start and end apart: 20 -> 22, of which waited for: 19 -> 20; matrix products, arithmetic and copies ran while one was open for 6% -> 9% of each run, Pallas kernels for 0% -> 0%
where the time goes in v1:
time: 914 us; the launch traced here: 905 us
  waiting for transfers between devices  490 us (54%)
  matrix products  167 us (18%)
  blocking collectives  84.3 us (9%)
  other arithmetic  75.9 us (8%)
  local copies, waits for them, and re-layouts  43 us (5%)
  starting transfers between devices  25.5 us (3%)
  between operations  19 us (2%)
    all_gather x1, waiting for transfers between devices, body(): lax.all_gather(w_down, 'dp', axis=2, tiled=True)  95.9 us
    all_gather x1, waiting for transfers between devices, body(): lax.all_gather(w_up, 'dp', axis=1, tiled=True)  95.9 us
    all_gather x1, waiting for transfers between devices, body(): lax.all_gather(w_gate, 'dp', axis=1, tiled=True)  75.1 us
    dot_general x7, matrix products, trunk_layer(): jnp.dot(hidden, down_weight, preferred_element_type=jnp.float32)  72.1 us
    reduce_scatter x7, waiting for transfers between devices, trunk_layer(): lax.psum_scatter(partial_out.astype(jnp.bfloat16), 'mp', scatter_dimensio...  60.3 us
    dot_general x14, matrix products, contract(): return jnp.einsum(form, left, right, preferred_element_type=jnp.float32)  56.3 us
    psum x1, waiting for transfers between devices, body(): lax.psum(grad_time.astype(jnp.bfloat16), ('dp', 'mp')).astype(jnp.float32)  48.8 us
    psum x1, waiting for transfers between devices, body(): lax.psum(lax.psum(grad_mid.astype(jnp.bfloat16), 'mp'), 'dp')  48.3 us
  transfers between devices with their start and end apart: 22, of which 20 were waited for; matrix products, arithmetic and copies ran while one was open for 9% of the time, Pallas kernels for 0%

profile of v1, /device:TPU:0, one launch (start us, length us, event | category | flops | bytes accessed | tf_op | source)
XLA Modules:
  0.0 904.7 jit_solution(7498700012790003516)
XLA Ops:
  14.4 6.5 concatenate.15
  20.9 4.2 fusion.91
  31.5 75.1 %all-gather.4.cloned.1.call-done = bf16[1,2560,1792]{2,1,0:T(8,128)(2,1)} async-done(((bf16[1,640,1792]{2,1,0:T(8,128)(2,1)}), bf16[1,2560,1792]{2,1,0:T(8,128)(2,1)}) %all-gather.4.cloned.1.call-update) | async-done | bytes 9175056 | tf_op jit(solution)/shard_map/all_gather | solution.py:156
  106.6 95.9 %all-gather.6.cloned.1.call-done = bf16[1,2560,1792]{2,1,0:T(8,128)(2,1)} async-done(((bf16[1,640,1792]{2,1,0:T(8,128)(2,1)}), bf16[1,2560,1792]{2,1,0:T(8,128)(2,1)}) %all-gather.6.cloned.1.call-update) | async-done | bytes 9175056 | tf_op jit(solution)/shard_map/all_gather | solution.py:157
  202.5 95.9 %all-gather.8.cloned.1.call-done = bf16[1,1792,2560]{2,1,0:T(8,128)(2,1)} async-done(((bf16[1,1792,640]{2,1,0:T(8,128)(2,1)}), bf16[1,1792,2560]{2,1,0:T(8,128)(2,1)}) %all-gather.8.cloned.1.call-update) | async-done | bytes 9175056 | tf_op jit(solution)/shard_map/all_gather | solution.py:158
  299.3 263.3 %while.17 = (s32[]{:T(128)}, bf16[64,1280]{1,0:T(8,128)(2,1)S(1)}, bf16[4,64,1280]{2,1,0:T(8,128)(2,1)}, pred[]{:T(512)}, bf16[4,64,1280]{2,1,0:T(8,128)(2,1)}, ...) while((s32[]{:T(128)}, bf16[64,1280]{1,0:T(8,128)(2,1)S(1)}, ...), condition=%wide.region_5.6_spmd, body=%wide.region_2.5_spmd.sunk | while | flops 1764835328 | bytes 34035272 | solution.py:202
  302.5 5.4 fusion.126
  307.9 10.3 %convolution_convert_fusion.5 = bf16[64,2560]{1,0:T(8,128)(2,1)} fusion(bf16[1792,2560]{1,0:T(8,128)(2,1)} %get-tuple-element.406, bf16[2560,1792]{1,0:T(8,128)(2,1)} %get-tuple-element.405, f32[64,1792]{1,0:T(8,128)S(1)} %fusion.126, bf16[64,2560]{1,0:T(8,128)(2,1)S(1)} %all_gather.35, f32[2560]{0:T(1024)S(1)} %get-tuple-element.403, ...), kind=kOutput, calls=%fused_computation.clone.1 | convolution fusion | flops 1175912448 | bytes 19474688 | tf_op jit(solution)/shard_map/while/body/eval_jaxpr/dot_general | solution.py:177
  319.2 7.0 reduce-scatter.5.cloned.1.call-done
  331.4 4.0 collective-permute-done
  338.5 5.4 fusion.126
  343.9 10.3 %convolution_convert_fusion.5 = bf16[64,2560]{1,0:T(8,128)(2,1)} fusion(bf16[1792,2560]{1,0:T(8,128)(2,1)} %get-tuple-element.406, bf16[2560,1792]{1,0:T(8,128)(2,1)} %get-tuple-element.405, f32[64,1792]{1,0:T(8,128)S(1)} %fusion.126, bf16[64,2560]{1,0:T(8,128)(2,1)S(1)} %all_gather.35, f32[2560]{0:T(1024)S(1)} %get-tuple-element.403, ...), kind=kOutput, calls=%fused_computation.clone.1 | convolution fusion | flops 1175912448 | bytes 19474688 | tf_op jit(solution)/shard_map/while/body/eval_jaxpr/dot_general | solution.py:177
  355.1 8.9 reduce-scatter.5.cloned.1.call-done
  369.3 3.9 collective-permute-done
  376.4 5.4 fusion.126
  381.8 10.3 %convolution_convert_fusion.5 = bf16[64,2560]{1,0:T(8,128)(2,1)} fusion(bf16[1792,2560]{1,0:T(8,128)(2,1)} %get-tuple-element.406, bf16[2560,1792]{1,0:T(8,128)(2,1)} %get-tuple-element.405, f32[64,1792]{1,0:T(8,128)S(1)} %fusion.126, bf16[64,2560]{1,0:T(8,128)(2,1)S(1)} %all_gather.35, f32[2560]{0:T(1024)S(1)} %get-tuple-element.403, ...), kind=kOutput, calls=%fused_computation.clone.1 | convolution fusion | flops 1175912448 | bytes 19474688 | tf_op jit(solution)/shard_map/while/body/eval_jaxpr/dot_general | solution.py:177
  393.0 8.9 reduce-scatter.5.cloned.1.call-done
  407.2 3.9 collective-permute-done
  414.3 5.4 fusion.126
  419.7 10.3 %convolution_convert_fusion.5 = bf16[64,2560]{1,0:T(8,128)(2,1)} fusion(bf16[1792,2560]{1,0:T(8,128)(2,1)} %get-tuple-element.406, bf16[2560,1792]{1,0:T(8,128)(2,1)} %get-tuple-element.405, f32[64,1792]{1,0:T(8,128)S(1)} %fusion.126, bf16[64,2560]{1,0:T(8,128)(2,1)S(1)} %all_gather.35, f32[2560]{0:T(1024)S(1)} %get-tuple-element.403, ...), kind=kOutput, calls=%fused_computation.clone.1 | convolution fusion | flops 1175912448 | bytes 19474688 | tf_op jit(solution)/shard_map/while/body/eval_jaxpr/dot_general | solution.py:177
  430.9 8.9 reduce-scatter.5.cloned.1.call-done
  445.1 3.9 collective-permute-done
  452.2 5.4 fusion.126
  457.5 10.3 %convolution_convert_fusion.5 = bf16[64,2560]{1,0:T(8,128)(2,1)} fusion(bf16[1792,2560]{1,0:T(8,128)(2,1)} %get-tuple-element.406, bf16[2560,1792]{1,0:T(8,128)(2,1)} %get-tuple-element.405, f32[64,1792]{1,0:T(8,128)S(1)} %fusion.126, bf16[64,2560]{1,0:T(8,128)(2,1)S(1)} %all_gather.35, f32[2560]{0:T(1024)S(1)} %get-tuple-element.403, ...), kind=kOutput, calls=%fused_computation.clone.1 | convolution fusion | flops 1175912448 | bytes 19474688 | tf_op jit(solution)/shard_map/while/body/eval_jaxpr/dot_general | solution.py:177
  468.8 8.9 reduce-scatter.5.cloned.1.call-done
  490.0 5.4 fusion.126
  495.4 10.3 %convolution_convert_fusion.5 = bf16[64,2560]{1,0:T(8,128)(2,1)} fusion(bf16[1792,2560]{1,0:T(8,128)(2,1)} %get-tuple-element.406, bf16[2560,1792]{1,0:T(8,128)(2,1)} %get-tuple-element.405, f32[64,1792]{1,0:T(8,128)S(1)} %fusion.126, bf16[64,2560]{1,0:T(8,128)(2,1)S(1)} %all_gather.35, f32[2560]{0:T(1024)S(1)} %get-tuple-element.403, ...), kind=kOutput, calls=%fused_computation.clone.1 | convolution fusion | flops 1175912448 | bytes 19474688 | tf_op jit(solution)/shard_map/while/body/eval_jaxpr/dot_general | solution.py:177
  506.7 8.9 reduce-scatter.5.cloned.1.call-done
  527.9 5.4 fusion.126
  533.3 10.3 %convolution_convert_fusion.5 = bf16[64,2560]{1,0:T(8,128)(2,1)} fusion(bf16[1792,2560]{1,0:T(8,128)(2,1)} %get-tuple-element.406, bf16[2560,1792]{1,0:T(8,128)(2,1)} %get-tuple-element.405, f32[64,1792]{1,0:T(8,128)S(1)} %fusion.126, bf16[64,2560]{1,0:T(8,128)(2,1)S(1)} %all_gather.35, f32[2560]{0:T(1024)S(1)} %get-tuple-element.403, ...), kind=kOutput, calls=%fused_computation.clone.1 | convolution fusion | flops 1175912448 | bytes 19474688 | tf_op jit(solution)/shard_map/while/body/eval_jaxpr/dot_general | solution.py:177
  544.6 8.9 reduce-scatter.5.cloned.1.call-done
  569.8 9.4 %all_gather.31 = bf16[64,1280]{1,0:T(8,128)(2,1)} all-gather(bf16[16,1280]{1,0:T(8,128)(2,1)S(1)} %fusion.57), channel_id=1, replica_groups=mesh['dp'=4,'segment'=4,'mp'=2] {'dp'}, dimensions={0}, use_global_device_ids=true | all-gather | bytes 204800 | tf_op jit(solution)/shard_map/all_gather | solution.py:249
  581.1 4.7 add_convert_fusion.3
  593.6 5.3 fusion.92
  602.5 5.3 fusion.28
  609.4 7.9 multiply_reduce_fusion.8
  622.0 5.0 add_convert_fusion.2
  627.0 7.7 fusion.30
  634.7 9.7 %fusion.45 = f32[64,64,1280]{2,1,0:T(8,128)} fusion(bf16[64,64,256]{2,1,0:T(8,128)(2,1)S(1)} %add_convert_fusion.2, bf16[1280,256]{1,0:T(8,128)(2,1)} %param.26), kind=kOutput, calls=%fused_computation.87 | convolution fusion | flops 2684354560 | bytes 23724032 | tf_op jit(solution)/shard_map/mhc,kc->mhk/dot_general | solution.py:36
  644.5 12.8 %fusion.88 = (f32[64,64,256]{2,1,0:T(8,128)S(1)}, f32[64,64,256]{2,1,0:T(8,128)S(1)}, f32[64,64,256]{2,1,0:T(8,128)}, f32[64,64,256]{2,1,0:T(8,128)}, f32[64,64,256]{2,1,0:T(8,128)}) fusion(f32[64,64,1280]{2,1,0:T(8,128)} %fusion.45), kind=kLoop, calls=%fused_computation.189 | loop fusion | bytes 41943040 | tf_op jit(solution)/shard_map/slice | solution.py:64
  657.4 13.4 %multiply_reduce_fusion = (f32[64,256]{1,0:T(8,128)S(1)}, f32[64,256]{1,0:T(8,128)}, f32[64,256]{1,0:T(8,128)}, f32[64,256]{1,0:T(8,128)S(1)}, f32[64,64,256]{2,1,0:T(8,128)}) fusion(f32[64,256]{1,0:T(8,128)S(1)} %copy.102, f32[64,64,256]{2,1,0:T(8,128)S(1)} %copy-done.2, f32[64,256]{1,0:T(8,128)S(1)} %copy.100, f32[64,256]{1,0:T(8,128)S(1)} %copy-done.12, ...), kind=kLoop, calls=%fused_computation.42 | loop fusion | flops 35586048 | bytes 29818880 | tf_op jit(solution)/shard_map/reduce_sum | solution.py:125
  673.3 8.4 all_gather.33
  696.7 48.8 %all-reduce.21.cloned.1.call-done = bf16[256,512]{1,0:T(8,128)(2,1)} async-done(((bf16[256,512]{1,0:T(8,128)(2,1)}), bf16[256,512]{1,0:T(8,128)(2,1)}) %all-reduce.21.cloned.1.call-update) | async-done | bytes 262160 | tf_op jit(solution)/shard_map/psum | solution.py:245
  746.2 48.3 %all-reduce.19.cloned.1.call-done = bf16[1280,256]{0,1:T(8,128)(2,1)} async-done(((bf16[1280,256]{0,1:T(8,128)(2,1)}), bf16[1280,256]{0,1:T(8,128)(2,1)}) %all-reduce.19.cloned.1.call-update) | async-done | bytes 655376 | tf_op jit(solution)/shard_map/psum | solution.py:242
  796.3 4.8 fusion.37
  801.1 25.4 %all-reduce.8 = (bf16[70,256]{0,1:T(8,128)(2,1)S(1)}, bf16[14,256]{1,0:T(8,128)(2,1)S(1)}, bf16[256,14]{0,1:T(8,128)(2,1)S(1)}, bf16[]{:T(256)}) all-reduce(bf16[70,256]{0,1:T(8,128)(2,1)S(1)} %fusion.37, bf16[14,256]{1,0:T(8,128)(2,1)S(1)} %copy-done.30, ...), channel_id=1, replica_groups=mesh['dp'=4,'segment'=4,'mp'=2] {'dp','mp'}, use_global_device_ids=true, to_apply=%region_28.30 | all-reduce | flops 25089 | bytes 100356 | tf_op jit(solution)/shard_map/psum | solution.py:241
  827.6 25.0 %all-reduce.24 = (bf16[70,256]{0,1:T(8,128)(2,1)S(1)}, bf16[14,256]{1,0:T(8,128)(2,1)S(1)}, bf16[256,14]{0,1:T(8,128)(2,1)S(1)}, bf16[16,1280]{1,0:T(8,128)(2,1)S(1)}, bf16[]{:T(256)}) all-reduce(bf16[70,256]{0,1:T(8,128)(2,1)S(1)} %broadcast_select_fusion.2, ...), channel_id=1, replica_groups=mesh['dp'=4,'segment'=4,'mp'=2] {'segment'}, use_global_device_ids=true, to_apply=%region_29.31 | all-reduce | flops 45569 | bytes 182276 | tf_op jit(solution)/shard_map/psum | solution.py:23
  855.9 35.6 %all-reduce.23.cloned.1.call-done = (bf16[1280,256]{0,1:T(8,128)(2,1)}, bf16[256,512]{1,0:T(8,128)(2,1)}, bf16[1280,512]{1,0:T(8,128)(2,1)}) async-done(((bf16[1280,256]{0,1:T(8,128)(2,1)}, bf16[256,512]{1,0:T(8,128)(2,1)}, bf16[1280,512]{1,0:T(8,128)(2,1)}), (bf16[1280,256]{0,1:T(8,128)(2,1)}, bf16[256,512]{1,0:T(8,128)(2,1)}, bf16[1280,512]{1,0:T(8,128)(2,1)})) %all-reduce.23.cloned.1.call-update) | async-done | bytes 2228240 | tf_op jit(solution)/shard_map/psum | solution.py:23
  (267 shorter events, 144.4 us)
Async XLA Ops:
  7.2 556.9 %copy-start = (bf16[1280,512]{1,0:T(8,128)(2,1)S(1)}, bf16[1280,512]{1,0:T(8,128)(2,1)}, u32[]{:S(2)}) copy-start(bf16[1280,512]{1,0:T(8,128)(2,1)} %param.23) | copy-start | bytes 3932164
  7.2 99.4 %all-gather.4.cloned.1.call-start = ((), (), s32[]{:S(2)}) async-start(), calls=%async_computation.2 | async-start | bytes 11468800 | tf_op jit(solution)/shard_map/all_gather | solution.py:156
  7.9 194.6 %all-gather.6.cloned.1.call-start = ((), (), s32[]{:S(2)}) async-start(), calls=%async_computation.3 | async-start | bytes 11468800 | tf_op jit(solution)/shard_map/all_gather | solution.py:157
  8.7 289.7 %all-gather.8.cloned.1.call-start = ((), (), s32[]{:S(2)}) async-start(), calls=%async_computation.4 | async-start | bytes 11468800 | tf_op jit(solution)/shard_map/all_gather | solution.py:158
  11.2 591.3 %copy-start.4 = (bf16[8,8,64,14]{3,2,1,0:T(8,128)(2,1)}, bf16[8,8,64,14]{3,2,1,0:T(8,128)(2,1)S(1)}, u32[]{:S(2)}) copy-start(bf16[8,8,64,14]{3,2,1,0:T(8,128)(2,1)S(1)} %copy.96) | copy-start | bytes 344068
  14.4 6.5 copy-start.29
  20.8 7.6 copy-start.32
  299.3 26.8 %reduce-scatter.5.cloned.1.call-start = ((), (), s32[]{:S(2)}) async-start(), calls=%async_computation.10 | async-start | bytes 491520 | tf_op jit(solution)/shard_map/while/body/eval_jaxpr/reduce_scatter | solution.py:178
  327.8 7.6 collective-permute-start
  335.3 28.7 %reduce-scatter.5.cloned.1.call-start = ((), (), s32[]{:S(2)}) async-start(), calls=%async_computation.10 | async-start | bytes 491520 | tf_op jit(solution)/shard_map/while/body/eval_jaxpr/reduce_scatter | solution.py:178
  365.7 7.5 collective-permute-start
  373.2 28.7 %reduce-scatter.5.cloned.1.call-start = ((), (), s32[]{:S(2)}) async-start(), calls=%async_computation.10 | async-start | bytes 491520 | tf_op jit(solution)/shard_map/while/body/eval_jaxpr/reduce_scatter | solution.py:178
  403.6 7.5 collective-permute-start
  411.1 28.7 %reduce-scatter.5.cloned.1.call-start = ((), (), s32[]{:S(2)}) async-start(), calls=%async_computation.10 | async-start | bytes 491520 | tf_op jit(solution)/shard_map/while/body/eval_jaxpr/reduce_scatter | solution.py:178
  441.5 7.5 collective-permute-start
  449.0 28.7 %reduce-scatter.5.cloned.1.call-start = ((), (), s32[]{:S(2)}) async-start(), calls=%async_computation.10 | async-start | bytes 491520 | tf_op jit(solution)/shard_map/while/body/eval_jaxpr/reduce_scatter | solution.py:178
  479.4 7.5 collective-permute-start
  486.9 28.7 %reduce-scatter.5.cloned.1.call-start = ((), (), s32[]{:S(2)}) async-start(), calls=%async_computation.10 | async-start | bytes 491520 | tf_op jit(solution)/shard_map/while/body/eval_jaxpr/reduce_scatter | solution.py:178
  517.2 7.5 collective-permute-start
  524.8 28.7 %reduce-scatter.5.cloned.1.call-start = ((), (), s32[]{:S(2)}) async-start(), calls=%async_computation.10 | async-start | bytes 491520 | tf_op jit(solution)/shard_map/while/body/eval_jaxpr/reduce_scatter | solution.py:178
  555.1 7.5 collective-permute-start
  562.7 16.5 %reduce-scatter.3.cloned.1.call-start = ((), (), s32[]{:S(2)}) async-start(), calls=%async_computation.5 | async-start | bytes 24576 | tf_op jit(solution)/shard_map/reduce_scatter | solution.py:209
  564.0 15.9 %copy-start.13 = (f32[16,1280]{1,0:T(8,128)}, f32[16,1280]{1,0:T(8,128)S(1)}, u32[]{:S(2)}) copy-start(f32[16,1280]{1,0:T(8,128)S(1)} %convert_reduce_fusion) | copy-start | bytes 245764
  565.0 128.1 %all-reduce.17.cloned.1.call-start = ((), (), s32[]{:S(2)}) async-start(), calls=%async_computation.6 | async-start | bytes 1310720 | tf_op jit(solution)/shard_map/psum | solution.py:242
  566.0 43.4 %copy-start.35 = (f32[64]{0:T(128)}, f32[64]{0:T(128)S(1)}, u32[]{:S(2)}) copy-start(f32[64]{0:T(128)S(1)} %mul.384) | copy-start | bytes 772
  581.1 6.7 copy-start.11
  599.1 18.5 %copy-start.10 = (f32[64,256]{1,0:T(8,128)}, f32[64,256]{1,0:T(8,128)S(1)}, u32[]{:S(2)}) copy-start(f32[64,256]{1,0:T(8,128)S(1)} %copy.104) | copy-start | bytes 196612
  602.5 6.9 copy-start.24
  602.5 6.9 copy-start.3
  607.8 9.5 %copy-start.7 = (bf16[64,64,256]{2,1,0:T(8,128)(2,1)}, bf16[64,64,256]{2,1,0:T(8,128)(2,1)S(1)}, u32[]{:S(2)}) copy-start(bf16[64,64,256]{2,1,0:T(8,128)(2,1)S(1)} %fusion.28) | copy-start | bytes 6291460
  609.4 7.9 copy-start.8
  644.5 12.9 %copy-start.12 = (f32[64,256]{1,0:T(8,128)S(1)}, f32[64,256]{1,0:T(8,128)}, u32[]{:S(2)}) copy-start(f32[64,256]{1,0:T(8,128)} %copy-done.11) | copy-start | bytes 196612
  644.5 101.0 %all-reduce.21.cloned.1.call-start = ((), (), s32[]{:S(2)}) async-start(), calls=%async_computation.8 | async-start | bytes 524288 | tf_op jit(solution)/shard_map/psum | solution.py:245
  644.5 12.8 %copy-start.2 = (f32[64,64,256]{2,1,0:T(8,128)S(1)}, f32[64,64,256]{2,1,0:T(8,128)}, u32[]{:S(2)}) copy-start(f32[64,64,256]{2,1,0:T(8,128)} %get-tuple-element.299) | copy-start | bytes 12582916
  657.4 25.5 %copy-start.28 = (f32[64,128]{1,0:T(8,128)S(1)}, f32[64,128]{1,0:T(8,128)}, u32[]{:S(2)}) copy-start(f32[64,128]{1,0:T(8,128)} %get-tuple-element.296) | copy-start | bytes 98308
  657.4 27.4 %copy-start.9 = (f32[64,64,14]{1,2,0:T(8,128)S(1)}, f32[64,64,14]{1,2,0:T(8,128)}, u32[]{:S(2)}) copy-start(f32[64,64,14]{1,2,0:T(8,128)} %copy-done.8) | copy-start | bytes 688132
  657.4 27.4 %copy-start.36 = (f32[64]{0:T(128)S(1)}, f32[64]{0:T(128)}, u32[]{:S(2)}) copy-start(f32[64]{0:T(128)} %copy-done.35) | copy-start | bytes 772
  673.3 9.5 %copy-start.26 = (bf16[16,512]{1,0:T(8,128)(2,1)}, bf16[16,512]{1,0:T(8,128)(2,1)S(1)}, u32[]{:S(2)}) copy-start(bf16[16,512]{1,0:T(8,128)(2,1)S(1)} %all_gather.32) | copy-start | bytes 49156
  681.8 8.8 copy-start.25
  682.9 9.2 %copy-start.16 = (f32[64,256]{1,0:T(8,128)}, f32[64,256]{1,0:T(8,128)S(1)}, u32[]{:S(2)}) copy-start(f32[64,256]{1,0:T(8,128)S(1)} %copy.115) | copy-start | bytes 196612
  684.8 7.4 copy-start.23
  687.0 7.2 copy-start.5
  690.5 104.1 %all-reduce.19.cloned.1.call-start = ((), (), s32[]{:S(2)}) async-start(), calls=%async_computation.7 | async-start | bytes 1310720 | tf_op jit(solution)/shard_map/psum | solution.py:242
  693.0 103.3 %copy-start.6 = (bf16[64,64,70]{2,1,0:T(8,128)(2,1)S(1)}, bf16[64,64,70]{2,1,0:T(8,128)(2,1)}, u32[]{:S(2)}) copy-start(bf16[64,64,70]{2,1,0:T(8,128)(2,1)} %concatenate.15) | copy-start | bytes 1720324
  693.1 198.5 %all-reduce.23.cloned.1.call-start = ((), (), s32[]{:S(2)}) async-start(), calls=%async_computation.9 | async-start | bytes 4456448 | tf_op jit(solution)/shard_map/psum | solution.py:23
  696.7 99.5 %copy-start.17 = (f32[64,256]{1,0:T(8,128)S(1)}, f32[64,256]{1,0:T(8,128)}, u32[]{:S(2)}) copy-start(f32[64,256]{1,0:T(8,128)} %copy-done.16) | copy-start | bytes 196612
  796.3 30.9 %copy-start.14 = (f32[16,1280]{1,0:T(8,128)S(1)}, f32[16,1280]{1,0:T(8,128)}, u32[]{:S(2)}) copy-start(f32[16,1280]{1,0:T(8,128)} %copy-done.13) | copy-start | bytes 245764
  796.3 30.9 %copy-start.27 = (bf16[16,512]{1,0:T(8,128)(2,1)S(1)}, bf16[16,512]{1,0:T(8,128)(2,1)}, u32[]{:S(2)}) copy-start(bf16[16,512]{1,0:T(8,128)(2,1)} %copy-done.26) | copy-start | bytes 49156
  (12 other events, 37.5 us)
Sparse Core Ops, SparseCore 0:
  9.9 96.7 all-gather.3
  108.5 94.0 all-gather.5
  204.4 94.0 all-gather.7
  318.3 7.7 reduce-scatter.4
  354.3 9.6 reduce-scatter.4
  392.2 9.6 reduce-scatter.4
  430.1 9.6 reduce-scatter.4
  468.0 9.6 reduce-scatter.4
  505.9 9.6 reduce-scatter.4
  543.8 9.6 reduce-scatter.4
  566.2 9.4 reduce-scatter.2
  644.6 19.7 all-reduce.16
  690.6 54.8 all-reduce.20
  748.4 46.1 all-reduce.18
  797.6 93.9 all-reduce.22
